TPU v7x, 32 devices: a whole 2x2x4 slice. The times are simulated.
32 devices in a mesh: groups: 2 (over y), seq: 4 (over z), mp: 4 (over x, core).
Axes of the slice: x: 2, y: 2, z: 4, core: 2. Of those that a mesh axis runs over, the one named last changes fastest.
Arguments:
- nucleotide_features: bfloat16 [3072, 1536], P(('groups', 'seq')), parts along dimension 0, may hold values from -36 to 36
- location_table: bfloat16 [1536, 1536], P('seq'), may hold values from -6 to 6
- premix_rescaler: float32 [1536], replicated, may hold values from 0.5 to 1.5
- probe_lookup_matrices: bfloat16 [2, 1536, 1024], P(None, None, 'mp'), may hold values from -0.15625 to 0.15625
- payload_projector: bfloat16 [1536, 1536], P(None, 'mp'), may hold values from -0.15625 to 0.15625
- logit_sharpness: float32 [8], P('mp'), may hold values from 8 to 32
- mixing_projector: bfloat16 [1536, 1536], P('mp'), may hold values from -0.15625 to 0.15625
- premlp_rescaler: float32 [1536], replicated, may hold values from 0.5 to 1.5
- widening_matrix: bfloat16 [1536, 3072], P(None, 'mp'), may hold values from -0.15625 to 0.15625
- narrowing_matrix: bfloat16 [3072, 1536], P('mp'), may hold values from -0.109375 to 0.109375
Outputs:
- averaged: float32 [3072, 1536], P(('groups', 'seq'), 'mp'), parts along dimension 0
There are 2 independent parts, one for each index of `groups`. A program takes and returns all parts, laid end to end along the dimension named above; an argument that names none is the same for every part. Nothing has to cross between parts.
All inputs are finite; a program needn't handle non-finite values.
Results may differ from a plain program's by a relative error of at most 0.0033.
Values may be sent and summed in bfloat16 or wider, within the bound.
A program may use at most 128 MiB of HBM per device.

v0:
```python
import jax
import jax.numpy as jnp
from jax import lax
from jax.sharding import PartitionSpec as P

epsilon = 1e-06


def swapped(block, axis, apart):
    count = lax.axis_size(axis)
    route = []
    for low in range(count):
        high = low | 1 << apart
        if high != low and high < count:
            route += [(low, high), (high, low)]
    return lax.ppermute(block, axis, route)


def normalize(payload_vectors):
    return payload_vectors * lax.rsqrt(
        jnp.mean(payload_vectors * payload_vectors, axis=-1, keepdims=True) + epsilon
    )


def mirror_rows(block_rows):
    moved = block_rows
    for bit_index in range(lax.axis_size("seq").bit_length() - 1):
        moved = swapped(moved, "seq", bit_index)
    return jnp.flip(moved, 0)


def mirror_back(block_rows):
    moved = block_rows
    for bit_index in range(lax.axis_size("seq").bit_length() - 1):
        moved = swapped(moved, "seq", bit_index)
    return jnp.flip(moved, 0)


def shards(
    nucleotide_features,
    location_table,
    premix_rescaler,
    probe_lookup_matrices,
    payload_projector,
    logit_sharpness,
    mixing_projector,
    premlp_rescaler,
    widening_matrix,
    narrowing_matrix,
):
    rows_here = nucleotide_features.shape[0]
    width = nucleotide_features.shape[1]
    subspace_results = logit_sharpness.shape[0]
    lookup_dimension = probe_lookup_matrices.shape[2] // subspace_results
    value_size = payload_projector.shape[1] // subspace_results
    plus_sequence = nucleotide_features.astype(jnp.float32) + location_table.astype(jnp.float32)
    complement_sequence = mirror_rows(nucleotide_features).astype(
        jnp.float32
    ) + location_table.astype(jnp.float32)
    running_sum_hidden = jnp.stack([plus_sequence, complement_sequence])
    normed = (normalize(running_sum_hidden) * premix_rescaler).astype(jnp.bfloat16)
    query = jnp.einsum(
        "tsd,de->tse", normed, probe_lookup_matrices[0], preferred_element_type=jnp.float32
    )
    keys = jnp.einsum(
        "tsd,de->tse", normed, probe_lookup_matrices[1], preferred_element_type=jnp.float32
    )
    probe_unit_vectors = normalize(
        query.reshape(2, rows_here, subspace_results, lookup_dimension)
    ).astype(jnp.bfloat16)
    lookup_unit_vectors = normalize(
        keys.reshape(2, rows_here, subspace_results, lookup_dimension)
    ).astype(jnp.bfloat16)
    payload_vectors = jnp.einsum(
        "tsd,de->tse", normed, payload_projector, preferred_element_type=jnp.float32
    )
    payload_vectors = payload_vectors.astype(jnp.bfloat16).reshape(
        2, rows_here, subspace_results, value_size
    )
    logit_multiplier = logit_sharpness / lookup_dimension
    key_piece = lax.all_gather(lookup_unit_vectors, "seq", axis=1, tiled=True)
    value_piece = lax.all_gather(payload_vectors, "seq", axis=1, tiled=True)
    scores = jnp.einsum(
        "tqhe,tkhe->thqk", probe_unit_vectors, key_piece, preferred_element_type=jnp.float32
    )
    weight_exp = jnp.exp(scores * logit_multiplier[None, :, None, None])
    totals = jnp.sum(weight_exp, axis=-1)
    numer = jnp.einsum(
        "thqk,tkhe->tqhe",
        weight_exp.astype(jnp.bfloat16),
        value_piece,
        preferred_element_type=jnp.float32,
    )
    numer, totals = (numer, totals)
    mixed_positions = (numer / jnp.transpose(totals, (0, 2, 1))[..., None]).astype(jnp.bfloat16)
    mixed_positions = mixed_positions.reshape(2, rows_here, subspace_results * value_size)
    partial_value = jnp.einsum(
        "tsv,vd->tsd", mixed_positions, mixing_projector, preferred_element_type=jnp.float32
    )
    share = width // lax.axis_size("mp")
    offset = lax.axis_index("mp") * share
    middle = running_sum_hidden + lax.psum(partial_value, "mp")
    normed_mid = (normalize(middle) * premlp_rescaler).astype(jnp.bfloat16)
    middle_share = lax.dynamic_slice_in_dim(middle, offset, share, 2)
    expanded = jnp.einsum(
        "tsd,df->tsf", normed_mid, widening_matrix, preferred_element_type=jnp.float32
    )
    expanded = jax.nn.gelu(expanded, approximate=True).astype(jnp.bfloat16)
    reduced = jnp.einsum(
        "tsf,fd->tsd", expanded, narrowing_matrix, preferred_element_type=jnp.float32
    )
    strand_out = middle_share + lax.psum_scatter(
        reduced.astype(jnp.bfloat16), "mp", scatter_dimension=2, tiled=True
    ).astype(jnp.float32)
    return 0.5 * (strand_out[0] + mirror_back(strand_out[1]))


def solution(mesh):
    return jax.shard_map(
        shards,
        mesh=mesh,
        in_specs=(
            P(("groups", "seq"), None),
            P("seq", None),
            P(),
            P(None, None, "mp"),
            P(None, "mp"),
            P("mp"),
            P("mp", None),
            P(),
            P(None, "mp"),
            P("mp", None),
        ),
        out_specs=P(("groups", "seq"), "mp"),
        check_vma=False,
    )
```

profile of v0, /device:TPU:0, one launch (start us, length us, event | category | flops | bytes accessed | tf_op | source)
XLA Modules:
  0.0 423.8 jit_solution(6057223312280661653)
XLA Ops:
  6.5 3.1 collective-permute-start
  9.6 26.3 %collective-permute-done = bf16[384,1536]{1,0:T(8,128)(2,1)} collective-permute-done((bf16[384,1536]{1,0:T(8,128)(2,1)}, bf16[384,1536]{1,0:T(8,128)(2,1)}, u32[]{:S(2)}, u32[]{:S(2)}) %collective-permute-start) | collective-permute-done | bytes 1179680 | tf_op jit(solution)/shard_map/ppermute | solution.py:16
  35.9 2.8 collective-permute-start.1
  38.6 2.4 slice_bitcast_fusion.1
  42.2 47.3 %collective-permute-done.1 = bf16[384,1536]{1,0:T(8,128)(2,1)} collective-permute-done((bf16[384,1536]{1,0:T(8,128)(2,1)}, bf16[384,1536]{1,0:T(8,128)(2,1)}, u32[]{:S(2)}, u32[]{:S(2)}) %collective-permute-start.1) | collective-permute-done | bytes 1179680 | tf_op jit(solution)/shard_map/ppermute | solution.py:16
  89.5 14.2 %rev.8 = bf16[384,1536]{1,0:T(8,128)(2,1)S(1)} reverse(bf16[384,1536]{1,0:T(8,128)(2,1)} %collective-permute-done.1), dimensions={0} | reverse | bytes 2359296 | tf_op jit(solution)/shard_map/jit(_flip)/rev | solution.py:29
  103.7 2.3 fusion.6
  111.0 4.0 convolution_convert_fusion.1
  116.3 2.7 multiply_reduce_fusion.3
  119.0 29.8 %all-gather.5.cloned.1.call-done = bf16[2,1536,2,128]{1,3,2,0:T(8,128)(2,1)} async-done(((bf16[2,384,2,128]{1,3,2,0:T(8,128)(2,1)}), bf16[2,1536,2,128]{1,3,2,0:T(8,128)(2,1)}) %all-gather.5.cloned.1.call-update) | async-done | bytes 1572880 | tf_op jit(solution)/shard_map/all_gather | solution.py:81
  148.8 7.0 %fusion = (f32[2,2,384]{2,1,0:T(2,128)S(1)}, f32[2,2,384,1536]{3,2,1,0:T(8,128)}) fusion(f32[2]{0:T(128)S(1)} %broadcast_multiply_fusion, bf16[2,1536,2,128]{1,3,2,0:T(8,128)(2,1)} %all-gather.5.cloned.1.call-done, f32[2,384,2,128]{1,3,2,0:T(8,128)S(1)} %get-tuple-element.14, f32[2,384,2]{1,2,0:T(2,128)S(1)} %add_rsqrt_fusion.1), kind=kOutput, calls=%fused_computation.1 | convolution fusion | flops 609090048 | bytes 11808776 | tf_op jit(solution)/shard_map/tqhe,tkhe->thqk/dot_general | solution.py:83
  155.7 44.3 %all-gather.3.cloned.1.call-done = bf16[2,1536,2,192]{1,3,2,0:T(8,128)(2,1)} async-done(((bf16[2,384,2,192]{1,3,2,0:T(8,128)(2,1)}), bf16[2,1536,2,192]{1,3,2,0:T(8,128)(2,1)}) %all-gather.3.cloned.1.call-update) | async-done | bytes 2359312 | tf_op jit(solution)/shard_map/all_gather | solution.py:82
  200.0 6.2 %divide_convert_fusion = bf16[2,384,2,192]{1,3,2,0:T(8,128)(2,1)S(1)} fusion(bf16[2,1536,2,192]{1,3,2,0:T(8,128)(2,1)} %all-gather.3.cloned.1.call-done, f32[2,2,384,1536]{3,2,1,0:T(8,128)} %get-tuple-element.16, f32[2]{0:T(128)S(1)} %broadcast_multiply_fusion, f32[2,384,2]{1,2,0:T(2,128)S(1)} %bitcast.77), kind=kOutput, calls=%fused_computation.40 | convolution fusion | flops 911278080 | bytes 12392456 | tf_op jit(solution)/shard_map/thqk,tkhe->tqhe/dot_general | solution.py:88
  206.2 3.6 fusion.30
  210.0 92.6 %all-reduce.2.cloned.1.call-done = f32[2,384,1536]{2,1,0:T(8,128)} async-done(((f32[2,384,1536]{2,1,0:T(8,128)}), f32[2,384,1536]{2,1,0:T(8,128)}) %all-reduce.2.cloned.1.call-update) | async-done | bytes 4718608 | tf_op jit(solution)/shard_map/psum | solution.py:102
  302.6 6.4 %multiply_reduce_fusion = (f32[2,384]{1,0:T(2,128)S(1)}, f32[2,384,1536]{2,1,0:T(8,128)}) fusion(f32[2,384,1536]{2,1,0:T(8,128)} %all-reduce.2.cloned.1.call-done, f32[1,384,1536]{2,1,0:T(8,128)} %copy-done.2, f32[1,384,1536]{2,1,0:T(8,128)} %copy-done.1), kind=kLoop, calls=%fused_computation.6 | loop fusion | flops 4717824 | bytes 14158848 | tf_op jit(solution)/shard_map/reduce_sum | solution.py:21
  309.0 9.4 %convolution_convert_fusion = bf16[2,384,1536]{2,1,0:T(8,128)(2,1)} fusion(bf16[768,1536]{1,0:T(8,128)(2,1)S(1)} %copy-done, bf16[1536,768]{1,0:T(8,128)(2,1)} %param.18, f32[2,384,1536]{2,1,0:T(8,128)} %get-tuple-element.6, f32[1536]{0:T(1024)S(1)} %copy-done.8, f32[2,384]{1,0:T(2,128)S(1)} %add_rsqrt_fusion.2), kind=kOutput, calls=%fused_computation.11 | convolution fusion | flops 3633905664 | bytes 11805696 | tf_op jit(solution)/shard_map/tsf,fd->tsd/dot_general | solution.py:109
  318.4 6.8 %copy.29 = bf16[2,384,1536]{1,0,2:T(2,128)(2,1)} copy(bf16[2,384,1536]{2,1,0:T(8,128)(2,1)} %convolution_convert_fusion) | data formatting | bytes 4718592
  325.2 3.6 copy.31
  328.9 33.1 %reduce-scatter.4.cloned.1.call-done = bf16[384,768]{1,0:T(8,128)(2,1)} async-done(((bf16[1536,768]{1,0:T(8,128)(2,1)}), bf16[384,768]{1,0:T(8,128)(2,1)}) %reduce-scatter.4.cloned.1.call-update) | async-done | bytes 589840
  368.9 13.4 %collective-permute-done.2 = f32[384,384]{1,0:T(8,128)S(1)} collective-permute-done((f32[384,384]{1,0:T(8,128)S(1)}, f32[384,384]{1,0:T(8,128)S(1)}, u32[]{:S(2)}, u32[]{:S(2)}) %collective-permute-start.2) | collective-permute-done | bytes 589856 | tf_op jit(solution)/shard_map/ppermute | solution.py:16
  382.3 2.4 collective-permute-start.3
  384.7 25.3 %collective-permute-done.3 = f32[384,384]{1,0:T(8,128)} collective-permute-done((f32[384,384]{1,0:T(8,128)S(1)}, f32[384,384]{1,0:T(8,128)}, u32[]{:S(2)}, u32[]{:S(2)}) %collective-permute-start.3) | collective-permute-done | bytes 589856 | tf_op jit(solution)/shard_map/ppermute | solution.py:16
  410.0 5.3 %rev.9 = f32[384,384]{1,0:T(8,128)} reverse(f32[384,384]{1,0:T(8,128)} %collective-permute-done.3), dimensions={0} | reverse | bytes 1179648 | tf_op jit(solution)/shard_map/jit(_flip)/rev | solution.py:36
  (45 shorter events, 16.5 us)
Async XLA Ops:
  6.5 302.4 %copy-start = (bf16[768,1536]{1,0:T(8,128)(2,1)S(1)}, bf16[768,1536]{1,0:T(8,128)(2,1)}, u32[]{:S(2)}) copy-start(bf16[768,1536]{1,0:T(8,128)(2,1)} %param.19) | copy-start | bytes 7077892
  6.5 142.2 %all-gather.5.cloned.1.call-start = ((), (), s32[]{:S(2)}) async-start(), calls=%async_computation.2 | async-start | bytes 1966080 | tf_op jit(solution)/shard_map/all_gather | solution.py:81
  6.5 29.3 %collective-permute-start = (bf16[384,1536]{1,0:T(8,128)(2,1)}, bf16[384,1536]{1,0:T(8,128)(2,1)}, u32[]{:S(2)}, u32[]{:S(2)}) collective-permute-start(bf16[384,1536]{1,0:T(8,128)(2,1)} %param.10), channel_id=1, source_target_pairs={{0,4},{4,0},{8,12},{12,8},{1,5},{5,1},{9,13},{13,9},{2,6},{6,2},{1... | collective-permute-start | bytes 3538952 | tf_op jit(solution)/shard_map/ppermute | solution.py:16
  35.9 53.6 %collective-permute-start.1 = (bf16[384,1536]{1,0:T(8,128)(2,1)}, bf16[384,1536]{1,0:T(8,128)(2,1)}, u32[]{:S(2)}, u32[]{:S(2)}) collective-permute-start(bf16[384,1536]{1,0:T(8,128)(2,1)} %collective-permute-done), channel_id=1, source_target_pairs={{0,8},{8,0},{4,12},{12,4},{1,9},{9,1},{5,13},{13,5},{2,10},{10,2},... | collective-permute-start | bytes 3538952 | tf_op jit(solution)/shard_map/ppermute | solution.py:16
  106.0 1.5 copy-start.1
  106.0 2.1 copy-start.2
  106.0 2.1 copy-start.7
  108.2 1.1 copy-start.6
  108.6 1.5 copy-start.4
  111.0 4.1 copy-start.3
  111.0 5.3 %copy-start.9 = (f32[2]{0:T(128)S(1)}, f32[2]{0:T(128)}, u32[]{:S(2)}) copy-start(f32[2]{0:T(128)} %param.15) | copy-start | bytes 28
  111.0 89.0 %all-gather.3.cloned.1.call-start = ((), (), s32[]{:S(2)}) async-start(), calls=%async_computation.1 | async-start | bytes 2949120 | tf_op jit(solution)/shard_map/all_gather | solution.py:82
  115.0 187.6 %all-reduce.2.cloned.1.call-start = ((), (), s32[]{:S(2)}) async-start(), calls=%async_computation.3 | async-start | bytes 9437184 | tf_op jit(solution)/shard_map/psum | solution.py:102
  200.0 6.2 %copy-start.5 = (bf16[384,1536]{1,0:T(8,128)(2,1)S(1)}, bf16[384,1536]{1,0:T(8,128)(2,1)}, u32[]{:S(2)}) copy-start(bf16[384,1536]{1,0:T(8,128)(2,1)} %param.16) | copy-start | bytes 3538948
  209.8 99.2 %copy-start.8 = (f32[1536]{0:T(1024)S(1)}, f32[1536]{0:T(1024)}, u32[]{:S(2)}) copy-start(f32[1536]{0:T(1024)} %param.17) | copy-start | bytes 18436
  209.8 152.2 %reduce-scatter.4.cloned.1.call-start = ((), (), s32[]{:S(2)}) async-start(), calls=%async_computation.4 | async-start | bytes 2949120
  367.3 15.0 %collective-permute-start.2 = (f32[384,384]{1,0:T(8,128)S(1)}, f32[384,384]{1,0:T(8,128)S(1)}, u32[]{:S(2)}, u32[]{:S(2)}) collective-permute-start(f32[384,384]{1,0:T(8,128)S(1)} %slice_bitcast_fusion.2), channel_id=1, source_target_pairs={{0,4},{4,0},{8,12},{12,8},{1,5},{5,1},{9,13},{13,9},{2,6},{6,2},{1... | collective-permute-start | bytes 1769480 | tf_op jit(solution)/shard_map/ppermute | solution.py:16
  382.3 27.7 %collective-permute-start.3 = (f32[384,384]{1,0:T(8,128)S(1)}, f32[384,384]{1,0:T(8,128)}, u32[]{:S(2)}, u32[]{:S(2)}) collective-permute-start(f32[384,384]{1,0:T(8,128)S(1)} %collective-permute-done.2), channel_id=1, source_target_pairs={{0,8},{8,0},{4,12},{12,4},{1,9},{9,1},{5,13},{13,5},{2,10},{10,2},... | collective-permute-start | bytes 1769480 | tf_op jit(solution)/shard_map/ppermute | solution.py:16
Sparse Core Ops, SparseCore 0:
  111.1 37.6 all-gather.4
  150.3 49.5 all-gather.2
  209.9 92.6 all-reduce.1
  329.0 32.9 reduce-scatter.3
where the time goes:
time: 426 us; the launch traced here: 424 us
  waiting for transfers between devices  312 us (73%)
  local copies, waits for them, and re-layouts  40.9 us (10%)
  matrix products  33.6 us (8%)
  other arithmetic  13.9 us (3%)
  between operations  13.3 us (3%)
  starting transfers between devices  10.1 us (2%)
    ppermute x4, waiting for transfers between devices, swapped(): return lax.ppermute(block, axis, route)  112 us
    psum x1, waiting for transfers between devices, shards(): middle = running_sum_hidden + lax.psum(partial_value, 'mp')  92.6 us
    all_gather x1, waiting for transfers between devices, shards(): value_piece = lax.all_gather(payload_vectors, 'seq', axis=1, tiled=True)  44.3 us
    unnamed x5, waiting for transfers between devices  33.2 us
    all_gather x1, waiting for transfers between devices, shards(): key_piece = lax.all_gather(lookup_unit_vectors, 'seq', axis=1, tiled=True)  29.8 us
    unnamed x24, local copies, waits for them, and re-layouts  16.6 us
    rev x1, local copies, waits for them, and re-layouts, mirror_rows(): return jnp.flip(moved, 0)  14.2 us
    ppermute x4, starting transfers between devices, swapped(): return lax.ppermute(block, axis, route)  9.78 us
  transfers between devices with their start and end apart: 8, of which 8 were waited for; matrix products, arithmetic and copies ran while one was open for 4% of the time, Pallas kernels for 0%

commit v1 on v0

v1 whole, which is shorter than its diff:
```python
import functools

import jax
import jax.numpy as jnp
from jax import lax
from jax.experimental import pallas as pl
from jax.experimental.pallas import tpu as pltpu
from jax.sharding import PartitionSpec as P

epsilon = 1e-06
MESH = pl.DeviceIdType.MESH
f32 = jnp.float32
bf16 = jnp.bfloat16


def normalize(v):
    return v * lax.rsqrt(jnp.mean(v * v, axis=-1, keepdims=True) + epsilon)


def gather_kernel(nz, nm, *refs):
    src = refs[0:2]
    out = refs[2:4]
    stage, lsem, zs, zr, xs, xr, cs, cr = refs[4:]
    nx = nm // 2
    z = lax.axis_index("seq")
    m = lax.axis_index("mp")
    x, c = m // 2, m % 2
    rows = src[0].shape[0]
    piece = rows // nm

    def at(zsrc, mm):
        return pl.ds(pl.multiple_of(zsrc * rows + mm * piece, piece), piece)

    others = [lax.rem(x + d, nx) for d in range(1, nx)]
    barrier = pltpu.get_barrier_semaphore()

    @pl.when(z > 0)
    def _():
        pl.semaphore_signal(barrier, inc=1, device_id={"seq": z - 1}, device_id_type=MESH)

    @pl.when(z < nz - 1)
    def _():
        pl.semaphore_signal(barrier, inc=1, device_id={"seq": z + 1}, device_id_type=MESH)

    for o in others:
        pl.semaphore_signal(barrier, inc=1, device_id={"mp": o * 2 + c}, device_id_type=MESH)
    pl.semaphore_signal(barrier, inc=1, device_id={"mp": x * 2 + 1 - c}, device_id_type=MESH)

    loads = [pltpu.make_async_copy(src[a], stage.at[a], lsem.at[a]) for a in range(2)]
    for cp in loads:
        cp.start()

    pl.semaphore_wait(barrier, nx + jnp.where(z > 0, 1, 0) + jnp.where(z < nz - 1, 1, 0))

    def zsend(a, dist, right):
        zsrc = z - dist if right else z + dist
        s = at(zsrc, m)
        if dist == 0:
            ref = src[a].at[pl.ds(pl.multiple_of(m * piece, piece), piece)]
        else:
            ref = out[a].at[s]
        k = 0 if right else 1
        return pltpu.make_async_remote_copy(
            src_ref=ref, dst_ref=out[a].at[s],
            send_sem=zs.at[a, k, dist], recv_sem=zr.at[a, k, dist],
            device_id={"seq": z + 1 if right else z - 1}, device_id_type=MESH)

    def zrecv(a, dist, right):
        zsrc = z - dist if right else z + dist
        s = at(zsrc, m)
        k = 0 if right else 1
        return pltpu.make_async_remote_copy(
            src_ref=out[a].at[s], dst_ref=out[a].at[s],
            send_sem=zs.at[a, k, dist - 1], recv_sem=zr.at[a, k, dist - 1],
            device_id={"seq": z + 1 if right else z - 1}, device_id_type=MESH)

    def xcopy(a, k, dist, d, right, mine):
        zsrc = z - dist if right else z + dist
        o = lax.rem(x + d, nx) if mine else lax.rem(x - d + nx, nx)
        s = at(zsrc, m if mine else o * 2 + c)
        return pltpu.make_async_remote_copy(
            src_ref=out[a].at[s], dst_ref=out[a].at[s],
            send_sem=xs.at[a, k, dist - 1, d - 1], recv_sem=xr.at[a, k, dist - 1, d - 1],
            device_id={"mp": o * 2 + c}, device_id_type=MESH)

    def ccopy(a, k, dist, d, right, mine):
        zsrc = z - dist if right else z + dist
        o = lax.rem(x - d + nx, nx)
        s = at(zsrc, o * 2 + (c if mine else 1 - c))
        return pltpu.make_async_remote_copy(
            src_ref=out[a].at[s], dst_ref=out[a].at[s],
            send_sem=cs.at[a, k, dist - 1, d], recv_sem=cr.at[a, k, dist - 1, d],
            device_id={"mp": x * 2 + 1 - c}, device_id_type=MESH)

    def when(cond, f):
        @pl.when(cond)
        def _():
            f()

    can = {True: z < nz - 1, False: z > 0}

    for a in range(2):
        for right in (True, False):
            when(can[right], lambda a=a, right=right: zsend(a, 0, right).start())
    for a in range(2):
        loads[a].wait()
        st = pltpu.make_async_copy(
            stage.at[a], out[a].at[pl.ds(pl.multiple_of(z * rows, rows), rows)], lsem.at[a])
        st.start()

    def has(dist, right):
        return z - dist >= 0 if right else z + dist <= nz - 1

    def zstep(dist):
        for a in range(2):
            for right in (True, False):
                k = 0 if right else 1

                def got(a=a, right=right, k=k):
                    zrecv(a, dist, right).wait_recv()
                    if dist < nz - 1:
                        when(can[right], lambda: zsend(a, dist, right).start())
                    for d in range(1, nx):
                        xcopy(a, k, dist, d, right, True).start()
                    ccopy(a, k, dist, 0, right, True).start()

                when(has(dist, right), got)

    def xstep(dist):
        for a in range(2):
            for right in (True, False):
                k = 0 if right else 1

                def got(a=a, right=right, k=k):
                    for d in range(1, nx):
                        xcopy(a, k, dist, d, right, False).wait_recv()
                        ccopy(a, k, dist, d, right, True).start()

                when(has(dist, right), got)

    for dist in range(1, nz):
        zstep(dist)
        if dist > 1:
            xstep(dist - 1)
    xstep(nz - 1)

    for a in range(2):
        pltpu.make_async_copy(
            stage.at[a], out[a].at[pl.ds(pl.multiple_of(z * rows, rows), rows)], lsem.at[a]).wait()
    for dist in range(0, nz):
        for a in range(2):
            for right in (True, False):
                k = 0 if right else 1
                if dist < nz - 1:
                    cond = can[right] if dist == 0 else has(dist, right) & can[right]
                    when(cond, lambda a=a, right=right: zsend(a, dist, right).wait_send())
                if dist > 0:
                    def fin(a=a, right=right, k=k):
                        for d in range(1, nx):
                            xcopy(a, k, dist, d, right, True).wait_send()
                        for d in range(nx):
                            ccopy(a, k, dist, d, right, True).wait_send()
                            ccopy(a, k, dist, d, right, False).wait_recv()
                    when(has(dist, right), fin)


def gather_inputs(nuc, loc, nz, nm):
    rows, width = nuc.shape
    nx = nm // 2
    dma = pltpu.SemaphoreType.DMA
    anyspec = pl.BlockSpec(memory_space=pl.ANY)
    shape = jax.ShapeDtypeStruct((nz * rows, width), bf16)
    return pl.pallas_call(
        functools.partial(gather_kernel, nz, nm),
        out_shape=(shape, shape),
        in_specs=[anyspec] * 2,
        out_specs=[anyspec] * 2,
        scratch_shapes=[
            pltpu.VMEM((2, rows, width), bf16),
            dma((2,)),
            dma((2, 2, nz)), dma((2, 2, nz)),
            dma((2, 2, nz - 1, nx)), dma((2, 2, nz - 1, nx)),
            dma((2, 2, nz - 1, nx)), dma((2, 2, nz - 1, nx)),
        ],
        compiler_params=pltpu.CompilerParams(collective_id=0, has_side_effects=True),
        name="gather_inputs",
    )(nuc, loc)


def attend_kernel(nz, heads, qk, vd, sharp, nuc, loc, gain, wqk, wv, out, q_s, k_s, v_s):
    t, j = pl.program_id(0), pl.program_id(1)
    z = lax.axis_index("seq")
    rows = nuc.shape[0]
    b = 128

    def body(flip):
        r_i = lax.broadcasted_iota(jnp.int32, (b, b), 0)
        c_i = lax.broadcasted_iota(jnp.int32, (b, b), 1)
        anti = jnp.where(r_i + c_i == b - 1, 1.0, 0.0).astype(bf16)
        parts = []
        nb = rows // b
        for i in range(nb):
            if flip:
                l = jnp.dot(anti, loc[(nb - 1 - i) * b:(nb - i) * b, :], preferred_element_type=f32)
            else:
                l = loc[i * b:(i + 1) * b, :].astype(f32)
            s = nuc[i * b:(i + 1) * b, :].astype(f32) + l
            parts.append((normalize(s) * gain[...]).astype(bf16))
        normed = jnp.concatenate(parts, axis=0)
        here = pl.ds(pl.multiple_of(j * rows, rows), rows)
        key = jnp.dot(normed, wqk[1], preferred_element_type=f32)
        for h in range(heads):
            k_s[here, h * qk:(h + 1) * qk] = normalize(key[:, h * qk:(h + 1) * qk]).astype(bf16)
        v_s[here, :] = jnp.dot(normed, wv[...], preferred_element_type=f32).astype(bf16)

        @pl.when(j == z)
        def _():
            query = jnp.dot(normed, wqk[0], preferred_element_type=f32)
            for h in range(heads):
                q_s[:, h * qk:(h + 1) * qk] = normalize(query[:, h * qk:(h + 1) * qk]).astype(bf16)

    @pl.when(t == 0)
    def _():
        body(False)

    @pl.when(t == 1)
    def _():
        body(True)

    @pl.when(j == nz - 1)
    def _():
        s_all = k_s.shape[0]
        chunk = 128
        wide = heads * vd
        for i in range(rows // chunk):
            rr = slice(i * chunk, (i + 1) * chunk)
            res = []
            for h in range(heads):
                lo = (h * vd) // 128 * 128
                hi = min(-(-((h + 1) * vd) // 128) * 128, wide)
                num = jnp.zeros((chunk, hi - lo), f32)
                tot = jnp.zeros((chunk, 1), f32)
                step = 1536
                for kk in range(0, s_all, step):
                    sc = lax.dot_general(
                        q_s[rr, h * qk:(h + 1) * qk], k_s[kk:kk + step, h * qk:(h + 1) * qk],
                        (((1,), (1,)), ((), ())), preferred_element_type=f32)
                    w = jnp.exp(sc * (sharp[h] / qk))
                    tot = tot + jnp.sum(w, axis=-1, keepdims=True)
                    num = num + jnp.dot(w.astype(bf16), v_s[kk:kk + step, lo:hi],
                                        preferred_element_type=f32)
                res.append((lo, hi, num / tot))
            if heads == 1:
                out[rr, :] = res[0][2].astype(bf16)
            else:
                for lo in range(0, wide, 128):
                    hi = min(lo + 128, wide)
                    col = lo + lax.broadcasted_iota(jnp.int32, (chunk, hi - lo), 1)
                    val = None
                    for h in range(heads):
                        l0, h0, r = res[h]
                        if h * vd < hi and (h + 1) * vd > lo:
                            v = r[:, lo - l0:hi - l0]
                            val = v if val is None else jnp.where(col < h * vd, val, v)
                    out[rr, lo:hi] = val.astype(bf16)


def attend(nuc_all, loc_all, gain, wqk, wv, sharp, nz, rows):
    heads = sharp.shape[0]
    width = nuc_all.shape[1]
    qk = wqk.shape[2] // heads
    vd = wv.shape[1] // heads
    s_all = nuc_all.shape[0]
    full = lambda a: pl.BlockSpec(a.shape, lambda t, j: (0,) * a.ndim, pipeline_mode=pl.Buffered(1))
    gain = gain.reshape(1, width)
    return pl.pallas_call(
        functools.partial(attend_kernel, nz, heads, qk, vd),
        grid=(2, nz),
        out_shape=jax.ShapeDtypeStruct((2, rows, heads * vd), bf16),
        in_specs=[
            pl.BlockSpec(memory_space=pltpu.SMEM),
            pl.BlockSpec((rows, width), lambda t, j: (j, 0)),
            pl.BlockSpec((rows, width), lambda t, j: (t * (nz - 1 - j) + (1 - t) * j, 0)),
            full(gain), full(wqk), full(wv),
        ],
        out_specs=pl.BlockSpec((pl.Squeezed(), rows, heads * vd), lambda t, j: (t, 0, 0)),
        scratch_shapes=[
            pltpu.VMEM((rows, heads * qk), bf16),
            pltpu.VMEM((s_all, heads * qk), bf16),
            pltpu.VMEM((s_all, heads * vd), bf16),
        ],
        compiler_params=pltpu.CompilerParams(vmem_limit_bytes=56 << 20),
        name="attend",
    )(sharp, nuc_all, loc_all, gain, wqk, wv)


def spread_kernel(nm, parts, src, out, lsem, xs, xr, cs, cr):
    nx = nm // 2
    m = lax.axis_index("mp")
    x, c = m // 2, m % 2
    n = src.shape[0] // parts
    barrier = pltpu.get_barrier_semaphore()
    for d in range(1, nx):
        pl.semaphore_signal(barrier, inc=1, device_id={"mp": lax.rem(x + d, nx) * 2 + c}, device_id_type=MESH)
    pl.semaphore_signal(barrier, inc=1, device_id={"mp": x * 2 + 1 - c}, device_id_type=MESH)
    local = pltpu.make_async_copy(src, out.at[m], lsem)
    local.start()
    pl.semaphore_wait(barrier, nx)

    def xcopy(i, d, mine):
        o = lax.rem(x + d, nx) if mine else lax.rem(x - d + nx, nx)
        k = m if mine else o * 2 + c
        r = pl.ds(i * n, n)
        return pltpu.make_async_remote_copy(
            src_ref=src.at[r], dst_ref=out.at[k, r], send_sem=xs.at[i, d - 1],
            recv_sem=xr.at[i, d - 1], device_id={"mp": o * 2 + c}, device_id_type=MESH)

    def ccopy(i, d, mine):
        o = lax.rem(x - d + nx, nx)
        k = o * 2 + (c if mine else 1 - c)
        r = pl.ds(i * n, n)
        ref = src.at[r] if d == 0 else out.at[k, r]
        return pltpu.make_async_remote_copy(
            src_ref=ref, dst_ref=out.at[k, r], send_sem=cs.at[i, d], recv_sem=cr.at[i, d],
            device_id={"mp": x * 2 + 1 - c}, device_id_type=MESH)

    for i in range(parts):
        for d in range(1, nx):
            xcopy(i, d, True).start()
    for i in range(parts):
        ccopy(i, 0, True).start()
    for i in range(parts):
        for d in range(1, nx):
            xcopy(i, d, False).wait_recv()
            ccopy(i, d, True).start()
    local.wait()
    for i in range(parts):
        for d in range(1, nx):
            xcopy(i, d, True).wait_send()
        for d in range(nx):
            ccopy(i, d, True).wait_send()
            ccopy(i, d, False).wait_recv()


def spread(a, nm, parts=4):
    nx = nm // 2
    dma = pltpu.SemaphoreType.DMA
    vm = pl.BlockSpec(memory_space=pltpu.VMEM)
    return pl.pallas_call(
        functools.partial(spread_kernel, nm, parts),
        out_shape=jax.ShapeDtypeStruct((nm,) + a.shape, a.dtype),
        in_specs=[vm],
        out_specs=vm,
        scratch_shapes=[dma, dma((parts, nx)), dma((parts, nx)), dma((parts, nx)), dma((parts, nx))],
        compiler_params=pltpu.CompilerParams(
            collective_id=1, has_side_effects=True, vmem_limit_bytes=40 << 20),
        name="spread",
    )(a)


def shards(nuc, loc, premix, wqk, wv, sharp, mixing, premlp, widen, narrow):
    rows, width = nuc.shape
    nz, nm = lax.axis_size("seq"), lax.axis_size("mp")
    z = lax.axis_index("seq")
    nuc_all, loc_all = gather_inputs(nuc, loc, nz, nm)
    mixing, nuc_all, loc_all = lax.optimization_barrier((mixing, nuc_all, loc_all))
    mix_all = lax.all_gather(mixing, "mp", axis=0, tiled=False)
    att = attend(nuc_all, loc_all, premix, wqk, wv, sharp, nz, rows)
    att_all = spread(att.reshape(2 * rows, -1), nm)
    loc_m = lax.dynamic_slice_in_dim(loc_all, (nz - 1 - z) * rows, rows, 0)
    i = lax.broadcasted_iota(jnp.int32, (rows, rows), 0)
    k = lax.broadcasted_iota(jnp.int32, (rows, rows), 1)
    anti = (i + k == rows - 1).astype(bf16)
    loc_rev = jnp.dot(anti, loc_m, preferred_element_type=f32)
    nf = nuc.astype(f32)
    stream = jnp.concatenate([nf + loc.astype(f32), nf + loc_rev], axis=0)
    proj = jnp.einsum("mrc,mcd->rd", att_all, mix_all, preferred_element_type=f32)
    middle = stream + proj
    normed_mid = (normalize(middle) * premlp).astype(bf16)
    up = jnp.dot(normed_mid, widen, preferred_element_type=f32)
    g = jax.nn.gelu(up, approximate=True)
    both = (g[:rows] + g[rows:]).astype(bf16)
    down = jnp.dot(both, narrow, preferred_element_type=f32)
    red = lax.psum_scatter(down.astype(bf16), "mp", scatter_dimension=1, tiled=True).astype(f32)
    share = width // nm
    mid = lax.dynamic_slice_in_dim(middle[:rows] + middle[rows:], lax.axis_index("mp") * share, share, 1)
    return 0.5 * (mid + red)


def solution(mesh):
    return jax.shard_map(
        shards,
        mesh=mesh,
        in_specs=(
            P(("groups", "seq"), None),
            P("seq", None),
            P(),
            P(None, None, "mp"),
            P(None, "mp"),
            P("mp"),
            P("mp", None),
            P(),
            P(None, "mp"),
            P("mp", None),
        ),
        out_specs=P(("groups", "seq"), "mp"),
        check_vma=False,
    )
```

time: 426 us -> 166 us (0.39)
  waiting for transfers between devices: 312 us -> 20.9 us
  Pallas kernels: 0 us -> 101 us
  local copies, waits for them, and re-layouts: 40.9 us -> 11.5 us
  matrix products: 33.6 us -> 14.5 us
  starting transfers between devices: 10.1 us -> 0.04 us
  other arithmetic: 13.9 us -> 3.93 us
    ppermute x4 -> x0, waiting for transfers between devices: 112 us -> none  [swapped(): return lax.ppermute(block, axis, route)]
    pallas_call x0 -> x3, Pallas kernels: none -> 101 us  [the longest x1 54 us: gather_inputs(): pl.pallas_call(functools.partial(gather_kernel, nz, nm), out_shape=(shape...]
    psum x1 -> x0, waiting for transfers between devices: 92.6 us -> none  [shards(): middle = running_sum_hidden + lax.psum(partial_value, 'mp')]
    all_gather x2 -> x1, waiting for transfers between devices: 74 us -> 0.01 us  [shards(): mix_all = lax.all_gather(mixing, 'mp', axis=0, tiled=False)]
    rev x2 -> x0, local copies, waits for them, and re-layouts: 19.5 us -> none  [the longest x1 14.2 us: mirror_rows(): return jnp.flip(moved, 0)]
    dot_general x7 -> x4, matrix products: 33.6 us -> 14.5 us  [the longest x1 7.42 us: shards(): jnp.einsum('mrc,mcd->rd', att_all, mix_all, preferred_element_type=f32)]
    unnamed x5 -> x3, waiting for transfers between devices: 33.2 us -> 20.9 us
    unnamed x24 -> x20, local copies, waits for them, and re-layouts: 16.6 us -> 6.03 us
  transfers between devices with their start and end apart: 8 -> 2, of which waited for: 8 -> 1; matrix products, arithmetic and copies ran while one was open for 4% -> 7% of each run, Pallas kernels for 0% -> 29%
where the time goes in v1:
time: 166 us
  Pallas kernels  101 us (61%)
  waiting for transfers between devices  20.9 us (13%)
  matrix products  14.5 us (9%)
  between operations  13.5 us (8%)
  local copies, waits for them, and re-layouts  11.5 us (7%)
  other arithmetic  3.93 us (2%)
    pallas_call x1, Pallas kernels, gather_inputs(): pl.pallas_call(functools.partial(gather_kernel, nz, nm), out_shape=(shape...  54 us
    pallas_call x1, Pallas kernels, spread(): pl.pallas_call(functools.partial(spread_kernel, nm, parts), out_shape=jax...  26.9 us
    unnamed x3, waiting for transfers between devices  20.9 us
    pallas_call x1, Pallas kernels, attend(): pl.pallas_call(functools.partial(attend_kernel, nz, heads, qk, vd), grid=...  20.4 us
    dot_general x1, matrix products, shards(): jnp.einsum('mrc,mcd->rd', att_all, mix_all, preferred_element_type=f32)  7.42 us
    unnamed x20, local copies, waits for them, and re-layouts  6.03 us
    slice x1, local copies, waits for them, and re-layouts, shards(): middle[:rows] + middle[rows:]  4.88 us
    dot_general x1, matrix products, shards(): loc_rev = jnp.dot(anti, loc_m, preferred_element_type=f32)  3.62 us
  transfers between devices with their start and end apart: 2, of which 1 were waited for; matrix products, arithmetic and copies ran while one was open for 7% of the time, Pallas kernels for 29%

profile of v1, /device:TPU:0, one launch (start us, length us, event | category | flops | bytes accessed | tf_op | source)
XLA Modules:
  0.0 165.7 jit_solution(5227247538654025887)
XLA Ops:
  6.5 54.0 %gather_inputs.1 = (bf16[1536,1536]{1,0:T(8,128)(2,1)}, bf16[1536,1536]{1,0:T(8,128)(2,1)}) custom-call(bf16[384,1536]{1,0:T(8,128)(2,1)} %refs_0_.1, bf16[384,1536]{1,0:T(8,128)(2,1)} %refs_1_.1), custom_call_target="tpu_custom_call" | custom-call | tf_op jit(solution)/shard_map/gather_inputs/pallas_call | solution.py:173
  60.5 0.0 all-gather.3.cloned.1.call-update
  60.5 0.0 reduce-scatter.4.cloned.1.call-start
  60.6 0.0 copy-done.6
  60.6 0.6 reshape.15.gain
  61.2 20.4 %attend.1 = bf16[2,384,384]{2,1,0:T(8,128)(2,1)} custom-call(f32[2]{0:T(128)} %sharp.1, bf16[1536,1536]{1,0:T(8,128)(2,1)} %get-tuple-element.13.nuc, bf16[1536,1536]{1,0:T(8,128)(2,1)} %get-tuple-element.12.loc, f32[1,1536]{1,0:T(1,128)} %reshape.15.gain, bf16[2,1536,256]{2,1,0:T(8,128)(2,1)} %wqk.1, bf16[1536,384]{1,0:T(8,128)(2,1)} %wv.1), custom_call_target="tpu_custom_call" | custom-call | tf_op jit(solution)/shard_map/attend/pallas_call | solution.py:276
  81.6 1.1 copy-done.1
  82.7 26.9 %spread.1 = bf16[4,768,384]{2,1,0:T(8,128)(2,1)S(1)} custom-call(bf16[768,384]{1,0:T(8,128)(2,1)S(1)} %bitcast.10), custom_call_target="tpu_custom_call" | custom-call | tf_op jit(solution)/shard_map/spread/pallas_call | solution.py:349
  109.6 0.0 copy-start.2
  109.6 1.4 copy-done.2
  111.0 3.6 %convolution_add_fusion = f32[384,1536]{1,0:T(8,128)} fusion(bf16[384,1536]{1,0:T(8,128)(2,1)S(1)} %copy-done.3, bf16[1536,1536]{1,0:T(8,128)(2,1)} %get-tuple-element.12.loc, s32[]{:T(128)S(6)} %select_n.6), kind=kOutput, calls=%fused_computation.4 | convolution fusion | flops 454459392 | bytes 4718596 | tf_op jit(solution)/shard_map/dot_general | solution.py:374
  114.6 1.8 %convert_add_fusion = f32[384,1536]{1,0:T(8,128)} fusion(bf16[384,1536]{1,0:T(8,128)(2,1)S(1)} %copy-done.3, bf16[384,1536]{1,0:T(8,128)(2,1)S(1)} %copy-done.5), kind=kLoop, calls=%fused_computation.5 | loop fusion | flops 1769472 | bytes 4718592 | tf_op jit(solution)/shard_map/add | solution.py:376
  116.4 7.4 %multiply_reduce_fusion = (f32[768]{0:T(1024)S(1)}, f32[768,1536]{1,0:T(8,128)S(1)}) fusion(bf16[4,768,384]{2,1,0:T(8,128)(2,1)} %copy-done.2, bf16[4,384,1536]{2,1,0:T(8,128)(2,1)} %bitcast.13, f32[384,1536]{1,0:T(8,128)} %convolution_add_fusion, f32[384,1536]{1,0:T(8,128)} %convert_add_fusion), kind=kOutput, calls=%fused_computation.2 | convolution fusion | flops 3628596480 | bytes 16518144 | tf_op jit(solution)/shard_map/mrc,mcd->rd/dot_general | solution.py:377
  123.8 0.0 copy-start.4
  123.9 0.0 copy-start.7
  123.9 2.4 %fusion.6 = f32[768,768]{1,0:T(8,128)S(1)} fusion(bf16[1536,768]{1,0:T(8,128)(2,1)S(1)} %copy-done, f32[768,1536]{1,0:T(8,128)S(1)} %get-tuple-element.18, f32[1536]{0:T(1024)S(1)} %copy-done.8, f32[768]{0:T(1024)S(1)} %add_rsqrt_fusion), kind=kOutput, calls=%fused_computation.13 | convolution fusion | flops 1820196864 | bytes 9446400 | tf_op jit(solution)/shard_map/dot_general | solution.py:380
  126.3 1.0 copy-done.7
  127.2 1.1 convolution_convert_fusion
  128.3 1.4 copy.11
  129.8 0.0 reduce-scatter.4.cloned.1.call-update
  129.8 4.9 %fusion.18 = (f32[384,1536]{1,0:T(8,128)}, f32[384,1536]{1,0:T(8,128)}) fusion(f32[768,1536]{1,0:T(8,128)} %copy-done.4), kind=kLoop, calls=%fused_computation.28 | loop fusion | bytes 9437184 | tf_op jit(solution)/shard_map/slice | solution.py:386
  134.7 20.9 %reduce-scatter.4.cloned.1.call-done = bf16[384,384]{1,0:T(8,128)(2,1)} async-done(((bf16[1536,384]{1,0:T(8,128)(2,1)}), bf16[384,384]{1,0:T(8,128)(2,1)}) %reduce-scatter.4.cloned.1.call-update) | async-done | bytes 294928
  155.6 1.2 copy.12
  156.7 2.1 %fusion.14 = f32[384,384]{1,0:T(8,128)} fusion(f32[384,1536]{1,0:T(8,128)} %get-tuple-element.16, s32[]{:T(128)S(6)} %select_n.7, f32[384,1536]{1,0:T(8,128)} %get-tuple-element.15, bf16[384,384]{1,0:T(8,128)(2,1)S(1)} %copy.12), kind=kLoop, calls=%fused_computation.22 | loop fusion | flops 589824 | bytes 2064388 | tf_op jit(solution)/shard_map/mul | solution.py:387
  (14 shorter events, 0.0 us)
Async XLA Ops:
  6.5 117.3 %copy-start = (bf16[1536,768]{1,0:T(8,128)(2,1)S(1)}, bf16[1536,768]{1,0:T(8,128)(2,1)}, u32[]{:S(2)}) copy-start(bf16[1536,768]{1,0:T(8,128)(2,1)} %param.18) | copy-start | bytes 7077892
  6.5 54.1 %copy-start.6 = (f32[1536]{0:T(1024)S(1)}, f32[1536]{0:T(1024)}, u32[]{:S(2)}) copy-start(f32[1536]{0:T(1024)} %param.12) | copy-start | bytes 18436
  6.5 109.9 %all-gather.3.cloned.1.call-start = ((), (), s32[]{:S(2)}) async-start(), calls=%async_computation.1 | async-start | bytes 5898240 | tf_op jit(solution)/shard_map/all_gather | solution.py:367
  60.5 95.0 %reduce-scatter.4.cloned.1.call-start = ((), (), s32[]{:S(2)}) async-start(), calls=%async_computation.2 | async-start | bytes 1474560
  81.6 1.1 copy-start.1
  82.7 28.3 %copy-start.3 = (bf16[384,1536]{1,0:T(8,128)(2,1)S(1)}, bf16[384,1536]{1,0:T(8,128)(2,1)}, u32[]{:S(2)}) copy-start(bf16[384,1536]{1,0:T(8,128)(2,1)} %refs_0_.1) | copy-start | bytes 3538948
  109.6 1.4 copy-start.2
  111.0 3.6 %copy-start.5 = (bf16[384,1536]{1,0:T(8,128)(2,1)S(1)}, bf16[384,1536]{1,0:T(8,128)(2,1)}, u32[]{:S(2)}) copy-start(bf16[384,1536]{1,0:T(8,128)(2,1)} %refs_1_.1) | copy-start | bytes 3538948
  116.4 7.5 %copy-start.8 = (f32[1536]{0:T(1024)S(1)}, f32[1536]{0:T(1024)}, u32[]{:S(2)}) copy-start(f32[1536]{0:T(1024)} %param.17) | copy-start | bytes 18436
  123.8 2.4 %copy-start.4 = (f32[768,1536]{1,0:T(8,128)}, f32[768,1536]{1,0:T(8,128)S(1)}, u32[]{:S(2)}) copy-start(f32[768,1536]{1,0:T(8,128)S(1)} %get-tuple-element.18) | copy-start | bytes 14155780
  123.9 3.3 %copy-start.7 = (bf16[768,1536]{1,0:T(8,128)(2,1)S(1)}, bf16[768,1536]{1,0:T(8,128)(2,1)}, u32[]{:S(2)}) copy-start(bf16[768,1536]{1,0:T(8,128)(2,1)} %param.19) | copy-start | bytes 7077892
Sparse Core Ops, SparseCore 0:
  60.7 46.6 all-gather.2
  129.9 25.6 reduce-scatter.3

commit v2 on v1

--- a/solution.py
+++ b/solution.py
@@ -187,7 +187,9 @@
     )(nuc, loc)
 
 
-def attend_kernel(nz, heads, qk, vd, sharp, nuc, loc, gain, wqk, wv, out, q_s, k_s, v_s):
+def attend_kernel(nz, nm, heads, qk, vd, sharp, nuc, loc, gain, wqk, wv, mix, out, mix_all,
+                  q_s, k_s, v_s, xs, xr, ys, yr, cs, cr, os, orr):
+    share_mix(nz, nm, mix, mix_all, xs, xr, ys, yr, cs, cr, os, orr, 0)
     t, j = pl.program_id(0), pl.program_id(1)
     z = lax.axis_index("seq")
     rows = nuc.shape[0]
@@ -264,127 +266,274 @@
                             val = v if val is None else jnp.where(col < h * vd, val, v)
                     out[rr, lo:hi] = val.astype(bf16)
 
-
-def attend(nuc_all, loc_all, gain, wqk, wv, sharp, nz, rows):
+    share_mix(nz, nm, mix, mix_all, xs, xr, ys, yr, cs, cr, os, orr, 1)
+
+
+def share_mix(nz, nm, mix, mix_all, xs, xr, ys, yr, cs, cr, os, orr, phase):
+    nx = nm // 2
+    step = pl.program_id(0) * nz + pl.program_id(1)
+    m = lax.axis_index("mp")
+    g = lax.axis_index("groups")
+    x, c = m // 2, m % 2
+    size = mix.shape[0] // 4
+
+    def rows(gg, p):
+        return pl.ds(pl.multiple_of((gg * 2 + p) * size, size), size)
+
+    def xcopy(p, d, mine):
+        o = lax.rem(x + d, nx) if mine else lax.rem(x - d + nx, nx)
+        k = m if mine else o * 2 + c
+        return pltpu.make_async_remote_copy(
+            src_ref=mix.at[rows(g, p)], dst_ref=mix_all.at[k, rows(g, p)],
+            send_sem=xs.at[p, d - 1], recv_sem=xr.at[p, d - 1],
+            device_id={"mp": o * 2 + c}, device_id_type=MESH)
+
+    def ycopy(p, d, mine):
+        k = lax.rem(x - d + nx, nx) * 2 + c
+        r = rows(g if mine else 1 - g, p)
+        return pltpu.make_async_remote_copy(
+            src_ref=mix_all.at[k, r], dst_ref=mix_all.at[k, r],
+            send_sem=ys.at[p, d - 1], recv_sem=yr.at[p, d - 1],
+            device_id={"groups": 1 - g}, device_id_type=MESH)
+
+    def ccopy(p, d, far, mine):
+        k = lax.rem(x - d + nx, nx) * 2 + (c if mine else 1 - c)
+        r = rows(1 - g if far else g, p)
+        f = 1 if far else 0
+        return pltpu.make_async_remote_copy(
+            src_ref=mix_all.at[k, r], dst_ref=mix_all.at[k, r],
+            send_sem=cs.at[p, d - 1, f], recv_sem=cr.at[p, d - 1, f],
+            device_id={"mp": x * 2 + 1 - c}, device_id_type=MESH)
+
+    def own(mine):
+        return pltpu.make_async_remote_copy(
+            src_ref=mix, dst_ref=mix_all.at[m if mine else x * 2 + 1 - c],
+            send_sem=os, recv_sem=orr,
+            device_id={"mp": x * 2 + 1 - c}, device_id_type=MESH)
+
+    if phase == 0:
+        @pl.when(step == 0)
+        def _():
+            barrier = pltpu.get_barrier_semaphore()
+            for d in range(1, nx):
+                pl.semaphore_signal(barrier, inc=1, device_id={"mp": lax.rem(x + d, nx) * 2 + c}, device_id_type=MESH)
+            pl.semaphore_signal(barrier, inc=1, device_id={"mp": x * 2 + 1 - c}, device_id_type=MESH)
+            pl.semaphore_signal(barrier, inc=1, device_id={"groups": 1 - g}, device_id_type=MESH)
+            pl.semaphore_wait(barrier, nx + 1)
+            for p in range(2):
+                for d in range(1, nx):
+                    xcopy(p, d, True).start()
+            own(True).start()
+
+        for p in range(2):
+            @pl.when(step == nz + 2 * p)
+            def _(p=p):
+                for d in range(1, nx):
+                    xcopy(p, d, False).wait_recv()
+                    ycopy(p, d, True).start()
+                    ccopy(p, d, False, True).start()
+    else:
+        @pl.when(step == 2 * nz - 1)
+        def _():
+            for p in range(2):
+                for d in range(1, nx):
+                    ycopy(p, d, False).wait_recv()
+                    ccopy(p, d, True, True).start()
+            own(True).wait_send()
+            own(False).wait_recv()
+            for p in range(2):
+                for d in range(1, nx):
+                    xcopy(p, d, True).wait_send()
+                    ycopy(p, d, True).wait_send()
+                    for far in (False, True):
+                        ccopy(p, d, far, True).wait_send()
+                        ccopy(p, d, far, False).wait_recv()
+
+
+def attend(nuc_all, loc_all, gain, wqk, wv, sharp, mix, nz, nm, rows):
     heads = sharp.shape[0]
     width = nuc_all.shape[1]
     qk = wqk.shape[2] // heads
     vd = wv.shape[1] // heads
     s_all = nuc_all.shape[0]
+    nx = nm // 2
+    dma = pltpu.SemaphoreType.DMA
     full = lambda a: pl.BlockSpec(a.shape, lambda t, j: (0,) * a.ndim, pipeline_mode=pl.Buffered(1))
+    anyspec = pl.BlockSpec(memory_space=pl.ANY)
     gain = gain.reshape(1, width)
     return pl.pallas_call(
-        functools.partial(attend_kernel, nz, heads, qk, vd),
+        functools.partial(attend_kernel, nz, nm, heads, qk, vd),
         grid=(2, nz),
-        out_shape=jax.ShapeDtypeStruct((2, rows, heads * vd), bf16),
+        out_shape=(jax.ShapeDtypeStruct((2, rows, heads * vd), bf16),
+                   jax.ShapeDtypeStruct((nm,) + mix.shape, bf16)),
         in_specs=[
             pl.BlockSpec(memory_space=pltpu.SMEM),
             pl.BlockSpec((rows, width), lambda t, j: (j, 0)),
             pl.BlockSpec((rows, width), lambda t, j: (t * (nz - 1 - j) + (1 - t) * j, 0)),
-            full(gain), full(wqk), full(wv),
+            full(gain), full(wqk), full(wv), anyspec,
         ],
-        out_specs=pl.BlockSpec((pl.Squeezed(), rows, heads * vd), lambda t, j: (t, 0, 0)),
+        out_specs=(pl.BlockSpec((pl.Squeezed(), rows, heads * vd), lambda t, j: (t, 0, 0)), anyspec),
         scratch_shapes=[
             pltpu.VMEM((rows, heads * qk), bf16),
             pltpu.VMEM((s_all, heads * qk), bf16),
             pltpu.VMEM((s_all, heads * vd), bf16),
+            dma((2, nx)), dma((2, nx)), dma((2, nx)), dma((2, nx)),
+            dma((2, nx, 2)), dma((2, nx, 2)), dma, dma,
         ],
-        compiler_params=pltpu.CompilerParams(vmem_limit_bytes=56 << 20),
+        compiler_params=pltpu.CompilerParams(
+            collective_id=2, has_side_effects=True, vmem_limit_bytes=56 << 20),
         name="attend",
-    )(sharp, nuc_all, loc_all, gain, wqk, wv)
-
-
-def spread_kernel(nm, parts, src, out, lsem, xs, xr, cs, cr):
+    )(sharp, nuc_all, loc_all, gain, wqk, wv, mix)
+
+
+def tail_kernel(nz, nm, att, nuc_h, loc_h, loc_all, gain, mix, mix_all, widen_h, narrow_h, out,
+                att_all, nuc, loc, locm, mixv, widen, narrow, sbuf, rbuf, mid,
+                lsem, msem, xs, xr, cs, cr, ss, sr):
     nx = nm // 2
+    rows, width = nuc.shape
+    share = width // nm
+    b = 128
+    parts = rows // b
+    z = lax.axis_index("seq")
     m = lax.axis_index("mp")
     x, c = m // 2, m % 2
-    n = src.shape[0] // parts
     barrier = pltpu.get_barrier_semaphore()
-    for d in range(1, nx):
-        pl.semaphore_signal(barrier, inc=1, device_id={"mp": lax.rem(x + d, nx) * 2 + c}, device_id_type=MESH)
-    pl.semaphore_signal(barrier, inc=1, device_id={"mp": x * 2 + 1 - c}, device_id_type=MESH)
-    local = pltpu.make_async_copy(src, out.at[m], lsem)
-    local.start()
-    pl.semaphore_wait(barrier, nx)
+    for d in range(1, nm):
+        pl.semaphore_signal(barrier, inc=1, device_id={"mp": lax.rem(m + d, nm)}, device_id_type=MESH)
+    loads = [
+        pltpu.make_async_copy(att, att_all.at[m], lsem.at[0]),
+        pltpu.make_async_copy(nuc_h, nuc, lsem.at[1]),
+        pltpu.make_async_copy(loc_h, loc, lsem.at[2]),
+        pltpu.make_async_copy(loc_all.at[pl.ds(pl.multiple_of((nz - 1 - z) * rows, rows), rows)], locm, lsem.at[3]),
+        pltpu.make_async_copy(widen_h, widen, lsem.at[4]),
+        pltpu.make_async_copy(narrow_h, narrow, lsem.at[5]),
+    ]
+    mloads = [pltpu.make_async_copy(mix, mixv.at[m], msem.at[0])]
+    for d in range(1, nm):
+        k = lax.rem(m + d, nm)
+        mloads.append(pltpu.make_async_copy(mix_all.at[k], mixv.at[k], msem.at[d]))
+    for cp in loads[:4] + mloads + loads[4:]:
+        cp.start()
+    pl.semaphore_wait(barrier, nm - 1)
 
     def xcopy(i, d, mine):
         o = lax.rem(x + d, nx) if mine else lax.rem(x - d + nx, nx)
         k = m if mine else o * 2 + c
-        r = pl.ds(i * n, n)
-        return pltpu.make_async_remote_copy(
-            src_ref=src.at[r], dst_ref=out.at[k, r], send_sem=xs.at[i, d - 1],
+        r = pl.ds(i * b, b)
+        return pltpu.make_async_remote_copy(
+            src_ref=att.at[:, r], dst_ref=att_all.at[k, :, r], send_sem=xs.at[i, d - 1],
             recv_sem=xr.at[i, d - 1], device_id={"mp": o * 2 + c}, device_id_type=MESH)
 
     def ccopy(i, d, mine):
         o = lax.rem(x - d + nx, nx)
         k = o * 2 + (c if mine else 1 - c)
-        r = pl.ds(i * n, n)
-        ref = src.at[r] if d == 0 else out.at[k, r]
-        return pltpu.make_async_remote_copy(
-            src_ref=ref, dst_ref=out.at[k, r], send_sem=cs.at[i, d], recv_sem=cr.at[i, d],
+        r = pl.ds(i * b, b)
+        ref = att.at[:, r] if d == 0 else att_all.at[k, :, r]
+        return pltpu.make_async_remote_copy(
+            src_ref=ref, dst_ref=att_all.at[k, :, r], send_sem=cs.at[i, d], recv_sem=cr.at[i, d],
             device_id={"mp": x * 2 + 1 - c}, device_id_type=MESH)
+
+    def scopy(i, d):
+        k = lax.rem(m + d, nm)
+        return pltpu.make_async_remote_copy(
+            src_ref=sbuf.at[i, k], dst_ref=rbuf.at[i, d - 1], send_sem=ss.at[i, d - 1],
+            recv_sem=sr.at[i, d - 1], device_id={"mp": k}, device_id_type=MESH)
 
     for i in range(parts):
         for d in range(1, nx):
             xcopy(i, d, True).start()
-    for i in range(parts):
         ccopy(i, 0, True).start()
-    for i in range(parts):
+
+    def pass_on(i):
         for d in range(1, nx):
             xcopy(i, d, False).wait_recv()
             ccopy(i, d, True).start()
-    local.wait()
+
+    r_i = lax.broadcasted_iota(jnp.int32, (b, b), 0)
+    c_i = lax.broadcasted_iota(jnp.int32, (b, b), 1)
+    anti = jnp.where(r_i + c_i == b - 1, 1.0, 0.0).astype(bf16)
+    for cp in loads[:4]:
+        cp.wait()
+    pass_on(0)
+    for cp in mloads:
+        cp.wait()
+    for i in range(parts):
+        r = slice(i * b, (i + 1) * b)
+        n = nuc[r, :].astype(f32)
+        s0 = n + loc[r, :].astype(f32)
+        s1 = n + jnp.dot(anti, locm[(parts - 1 - i) * b:(parts - i) * b, :], preferred_element_type=f32)
+        middle = jnp.concatenate([s0, s1], axis=0)
+        for d in range(nx):
+            ccopy(i, d, False).wait_recv()
+        for k in range(nm):
+            a = jnp.concatenate([att_all[k, 0, r, :], att_all[k, 1, r, :]], axis=0)
+            middle = middle + jnp.dot(a, mixv[k], preferred_element_type=f32)
+        if i + 1 < parts:
+            pass_on(i + 1)
+        normed = (normalize(middle) * gain[...]).astype(bf16)
+        if i == 0:
+            for cp in loads[4:]:
+                cp.wait()
+        up = jax.nn.gelu(jnp.dot(normed, widen[...], preferred_element_type=f32), approximate=True)
+        both = (up[:b] + up[b:]).astype(bf16)
+        down = jnp.dot(both, narrow[...], preferred_element_type=f32)
+        total = middle[:b] + middle[b:] + down
+        down = down.astype(bf16)
+        for k in range(nm):
+            sbuf[i, k] = down[:, k * share:(k + 1) * share]
+            mid[i, k] = total[:, k * share:(k + 1) * share]
+        for d in range(1, nm):
+            scopy(i, d).start()
+    for i in range(parts):
+        acc = mid[i, m]
+        for d in range(1, nm):
+            scopy(i, d).wait_recv()
+            acc = acc + rbuf[i, d - 1].astype(f32)
+        out[i * b:(i + 1) * b, :] = 0.5 * acc
     for i in range(parts):
         for d in range(1, nx):
             xcopy(i, d, True).wait_send()
         for d in range(nx):
             ccopy(i, d, True).wait_send()
-            ccopy(i, d, False).wait_recv()
-
-
-def spread(a, nm, parts=4):
+        for d in range(1, nm):
+            scopy(i, d).wait_send()
+
+
+def tail(att, nuc, loc, loc_all, gain, mix, mix_all, widen, narrow, nz, nm):
+    rows, width = nuc.shape
+    share = width // nm
     nx = nm // 2
+    parts = rows // 128
     dma = pltpu.SemaphoreType.DMA
+    anyspec = pl.BlockSpec(memory_space=pl.ANY)
     vm = pl.BlockSpec(memory_space=pltpu.VMEM)
+    v = pltpu.VMEM
     return pl.pallas_call(
-        functools.partial(spread_kernel, nm, parts),
-        out_shape=jax.ShapeDtypeStruct((nm,) + a.shape, a.dtype),
-        in_specs=[vm],
+        functools.partial(tail_kernel, nz, nm),
+        out_shape=jax.ShapeDtypeStruct((rows, share), f32),
+        in_specs=[vm, anyspec, anyspec, anyspec, vm, anyspec, anyspec, anyspec, anyspec],
         out_specs=vm,
-        scratch_shapes=[dma, dma((parts, nx)), dma((parts, nx)), dma((parts, nx)), dma((parts, nx))],
+        scratch_shapes=[
+            v((nm,) + att.shape, bf16), v(nuc.shape, bf16), v(nuc.shape, bf16), v(nuc.shape, bf16),
+            v((nm,) + mix.shape, bf16), v(widen.shape, bf16), v(narrow.shape, bf16),
+            v((parts, nm, 128, share), bf16), v((parts, nm - 1, 128, share), bf16),
+            v((parts, nm, 128, share), f32),
+            dma((6,)), dma((nm,)),
+            dma((parts, nx)), dma((parts, nx)), dma((parts, nx)), dma((parts, nx)),
+            dma((parts, nm)), dma((parts, nm)),
+        ],
         compiler_params=pltpu.CompilerParams(
-            collective_id=1, has_side_effects=True, vmem_limit_bytes=40 << 20),
-        name="spread",
-    )(a)
+            collective_id=3, has_side_effects=True, vmem_limit_bytes=56 << 20),
+        name="tail",
+    )(att, nuc, loc, loc_all, gain.reshape(1, width), mix, mix_all, widen, narrow)
 
 
 def shards(nuc, loc, premix, wqk, wv, sharp, mixing, premlp, widen, narrow):
-    rows, width = nuc.shape
+    rows = nuc.shape[0]
     nz, nm = lax.axis_size("seq"), lax.axis_size("mp")
-    z = lax.axis_index("seq")
     nuc_all, loc_all = gather_inputs(nuc, loc, nz, nm)
-    mixing, nuc_all, loc_all = lax.optimization_barrier((mixing, nuc_all, loc_all))
-    mix_all = lax.all_gather(mixing, "mp", axis=0, tiled=False)
-    att = attend(nuc_all, loc_all, premix, wqk, wv, sharp, nz, rows)
-    att_all = spread(att.reshape(2 * rows, -1), nm)
-    loc_m = lax.dynamic_slice_in_dim(loc_all, (nz - 1 - z) * rows, rows, 0)
-    i = lax.broadcasted_iota(jnp.int32, (rows, rows), 0)
-    k = lax.broadcasted_iota(jnp.int32, (rows, rows), 1)
-    anti = (i + k == rows - 1).astype(bf16)
-    loc_rev = jnp.dot(anti, loc_m, preferred_element_type=f32)
-    nf = nuc.astype(f32)
-    stream = jnp.concatenate([nf + loc.astype(f32), nf + loc_rev], axis=0)
-    proj = jnp.einsum("mrc,mcd->rd", att_all, mix_all, preferred_element_type=f32)
-    middle = stream + proj
-    normed_mid = (normalize(middle) * premlp).astype(bf16)
-    up = jnp.dot(normed_mid, widen, preferred_element_type=f32)
-    g = jax.nn.gelu(up, approximate=True)
-    both = (g[:rows] + g[rows:]).astype(bf16)
-    down = jnp.dot(both, narrow, preferred_element_type=f32)
-    red = lax.psum_scatter(down.astype(bf16), "mp", scatter_dimension=1, tiled=True).astype(f32)
-    share = width // nm
-    mid = lax.dynamic_slice_in_dim(middle[:rows] + middle[rows:], lax.axis_index("mp") * share, share, 1)
-    return 0.5 * (mid + red)
+    att, mix_all = attend(nuc_all, loc_all, premix, wqk, wv, sharp, mixing, nz, nm, rows)
+    return tail(att, nuc, loc, loc_all, premlp, mixing, mix_all, widen, narrow, nz, nm)
 
 
 def solution(mesh):

time: 166 us -> 117 us (0.70)
  waiting for transfers between devices: 20.9 us -> 0 us
  matrix products: 14.5 us -> 0 us
  between operations: 13.5 us -> 0.04 us
  Pallas kernels: 101 us -> 113 us
  local copies, waits for them, and re-layouts: 11.5 us -> 3.12 us
  other arithmetic: 3.93 us -> 0 us
    unnamed x3 -> x0, waiting for transfers between devices: 20.9 us -> none
    dot_general x4 -> x0, matrix products: 14.5 us -> none  [the longest x1 7.42 us: shards(): jnp.einsum('mrc,mcd->rd', att_all, mix_all, preferred_element_type=f32)]
    pallas_call x2, Pallas kernels: 47.3 us -> 59.4 us  [the longest x1 29.7 us: attend(): pl.pallas_call(functools.partial(attend_kernel, nz, nm, heads, qk, vd), g...]
    slice x1 -> x0, local copies, waits for them, and re-layouts: 4.88 us -> none  [shards(): middle[:rows] + middle[rows:]]
    unnamed x20 -> x5, local copies, waits for them, and re-layouts: 6.03 us -> 1.92 us
    mul x1 -> x0, other arithmetic: 2.15 us -> none  [shards(): return 0.5 * (mid + red)]
    add x1 -> x0, other arithmetic: 1.78 us -> none  [shards(): stream = jnp.concatenate([nf + loc.astype(f32), nf + loc_rev], axis=0)]
  transfers between devices with their start and end apart: 2 -> 0, of which waited for: 1 -> 0; matrix products, arithmetic and copies ran while one was open for 7% -> 0% of each run, Pallas kernels for 29% -> 0%
where the time goes in v2:
time: 117 us
  Pallas kernels  113 us (97%)
  local copies, waits for them, and re-layouts  3.12 us (3%)
    pallas_call x1, Pallas kernels, gather_inputs(): pl.pallas_call(functools.partial(gather_kernel, nz, nm), out_shape=(shape...  54 us
    pallas_call x1, Pallas kernels, attend(): pl.pallas_call(functools.partial(attend_kernel, nz, nm, heads, qk, vd), g...  29.7 us
    pallas_call x1, Pallas kernels, tail(): pl.pallas_call(functools.partial(tail_kernel, nz, nm), out_shape=jax.Shap...  29.7 us

profile of v2, /device:TPU:0, one launch (start us, length us, event | category | flops | bytes accessed | tf_op | source)
XLA Modules:
  0.0 116.5 jit_solution(12579449375122411903)
XLA Ops:
  0.0 0.0 copy-start
  0.0 54.0 %gather_inputs.1 = (bf16[1536,1536]{1,0:T(8,128)(2,1)}, bf16[1536,1536]{1,0:T(8,128)(2,1)}) custom-call(bf16[384,1536]{1,0:T(8,128)(2,1)} %nuc_h.1, bf16[384,1536]{1,0:T(8,128)(2,1)} %loc_h.1), custom_call_target="tpu_custom_call" | custom-call | tf_op jit(solution)/shard_map/gather_inputs/pallas_call | solution.py:173
  54.0 0.0 copy-done
  54.0 0.6 reshape.6.gain
  54.6 0.0 copy-start.1
  54.6 29.7 %attend.1 = (bf16[2,384,384]{2,1,0:T(8,128)(2,1)}, bf16[4,384,1536]{2,1,0:T(8,128)(2,1)}) custom-call(f32[2]{0:T(128)} %sharp.1, bf16[1536,1536]{1,0:T(8,128)(2,1)} %get-tuple-element.9.nuc, bf16[1536,1536]{1,0:T(8,128)(2,1)} %get-tuple-element.10.loc.loc_all, f32[1,1536]{1,0:T(1,128)} %reshape.6.gain, bf16[2,1536,256]{2,1,0:T(8,128)(2,1)} %wqk.1, ...), custom_call_target="tpu_custom_call" | custom-call | tf_op jit(solution)/shard_map/attend/pallas_call | solution.py:364
  84.3 0.0 copy-done.1
  84.3 0.6 reshape.7.gain
  84.9 29.7 %tail.1 = f32[384,384]{1,0:T(8,128)} custom-call(bf16[2,384,384]{2,1,0:T(8,128)(2,1)} %get-tuple-element.11.att, bf16[384,1536]{1,0:T(8,128)(2,1)} %nuc_h.1, bf16[384,1536]{1,0:T(8,128)(2,1)} %loc_h.1, bf16[1536,1536]{1,0:T(8,128)(2,1)} %get-tuple-element.10.loc.loc_all, f32[1,1536]{1,0:T(1,128)} %reshape.7.gain, bf16[384,1536]{1,0:T(8,128)(2,1)} %mix.3, ...), custom_call_target="tpu_custom_call" | custom-call | tf_op jit(solution)/shard_map/tail/pallas_call | solution.py:511
  114.6 1.9 %copy.12 = f32[384,384]{1,0:T(8,128)} copy(f32[384,384]{1,0:T(8,128)} %tail.1) | data formatting | bytes 1179648
Async XLA Ops:
  0.0 54.0 %copy-start = (f32[1536]{0:T(1024)S(1)}, f32[1536]{0:T(1024)}, u32[]{:S(2)}) copy-start(f32[1536]{0:T(1024)} %param.12) | copy-start | bytes 18436
  54.6 29.7 %copy-start.1 = (f32[1536]{0:T(1024)S(1)}, f32[1536]{0:T(1024)}, u32[]{:S(2)}) copy-start(f32[1536]{0:T(1024)} %param.17) | copy-start | bytes 18436

commit v3 on v2

--- a/solution.py
+++ b/solution.py
@@ -17,10 +17,15 @@
     return v * lax.rsqrt(jnp.mean(v * v, axis=-1, keepdims=True) + epsilon)
 
 
+def halves(rows, nm):
+    return rows // nm % 32 == 0
+
+
 def gather_kernel(nz, nm, *refs):
     src = refs[0:2]
     out = refs[2:4]
-    stage, lsem, zs, zr, xs, xr, cs, cr = refs[4:]
+    stage, lsem, zs, zr, xs, xr, cs, cr, ys, yr, fs, fr = refs[4:]
+    g = lax.axis_index("groups")
     nx = nm // 2
     z = lax.axis_index("seq")
     m = lax.axis_index("mp")
@@ -28,7 +33,13 @@
     rows = src[0].shape[0]
     piece = rows // nm
 
-    def at(zsrc, mm):
+    split = halves(rows, nm)
+    half = piece // 2
+
+    def at(a, zsrc, mm, peer=False):
+        if a == 1 and split:
+            gg = 1 - g if peer else g
+            return pl.ds(pl.multiple_of(zsrc * rows + mm * piece + gg * half, half), half)
         return pl.ds(pl.multiple_of(zsrc * rows + mm * piece, piece), piece)
 
     others = [lax.rem(x + d, nx) for d in range(1, nx)]
@@ -45,18 +56,20 @@
     for o in others:
         pl.semaphore_signal(barrier, inc=1, device_id={"mp": o * 2 + c}, device_id_type=MESH)
     pl.semaphore_signal(barrier, inc=1, device_id={"mp": x * 2 + 1 - c}, device_id_type=MESH)
+    if split:
+        pl.semaphore_signal(barrier, inc=1, device_id={"groups": 1 - g}, device_id_type=MESH)
 
     loads = [pltpu.make_async_copy(src[a], stage.at[a], lsem.at[a]) for a in range(2)]
     for cp in loads:
         cp.start()
 
-    pl.semaphore_wait(barrier, nx + jnp.where(z > 0, 1, 0) + jnp.where(z < nz - 1, 1, 0))
+    pl.semaphore_wait(barrier, nx + int(split) + jnp.where(z > 0, 1, 0) + jnp.where(z < nz - 1, 1, 0))
 
     def zsend(a, dist, right):
         zsrc = z - dist if right else z + dist
-        s = at(zsrc, m)
+        s = at(a, zsrc, m)
         if dist == 0:
-            ref = src[a].at[pl.ds(pl.multiple_of(m * piece, piece), piece)]
+            ref = src[a].at[at(a, 0, m)]
         else:
             ref = out[a].at[s]
         k = 0 if right else 1
@@ -67,7 +80,7 @@
 
     def zrecv(a, dist, right):
         zsrc = z - dist if right else z + dist
-        s = at(zsrc, m)
+        s = at(a, zsrc, m)
         k = 0 if right else 1
         return pltpu.make_async_remote_copy(
             src_ref=out[a].at[s], dst_ref=out[a].at[s],
@@ -77,7 +90,7 @@
     def xcopy(a, k, dist, d, right, mine):
         zsrc = z - dist if right else z + dist
         o = lax.rem(x + d, nx) if mine else lax.rem(x - d + nx, nx)
-        s = at(zsrc, m if mine else o * 2 + c)
+        s = at(a, zsrc, m if mine else o * 2 + c)
         return pltpu.make_async_remote_copy(
             src_ref=out[a].at[s], dst_ref=out[a].at[s],
             send_sem=xs.at[a, k, dist - 1, d - 1], recv_sem=xr.at[a, k, dist - 1, d - 1],
@@ -86,10 +99,26 @@
     def ccopy(a, k, dist, d, right, mine):
         zsrc = z - dist if right else z + dist
         o = lax.rem(x - d + nx, nx)
-        s = at(zsrc, o * 2 + (c if mine else 1 - c))
+        s = at(a, zsrc, o * 2 + (c if mine else 1 - c))
         return pltpu.make_async_remote_copy(
             src_ref=out[a].at[s], dst_ref=out[a].at[s],
             send_sem=cs.at[a, k, dist - 1, d], recv_sem=cr.at[a, k, dist - 1, d],
+            device_id={"mp": x * 2 + 1 - c}, device_id_type=MESH)
+
+    def ycopy(k, dist, d, right, mine):
+        zsrc = z - dist if right else z + dist
+        s = at(1, zsrc, lax.rem(x - d + nx, nx) * 2 + c, not mine)
+        return pltpu.make_async_remote_copy(
+            src_ref=out[1].at[s], dst_ref=out[1].at[s],
+            send_sem=ys.at[k, dist - 1, d], recv_sem=yr.at[k, dist - 1, d],
+            device_id={"groups": 1 - g}, device_id_type=MESH)
+
+    def fcopy(k, dist, d, right, mine):
+        zsrc = z - dist if right else z + dist
+        s = at(1, zsrc, lax.rem(x - d + nx, nx) * 2 + (c if mine else 1 - c), True)
+        return pltpu.make_async_remote_copy(
+            src_ref=out[1].at[s], dst_ref=out[1].at[s],
+            send_sem=fs.at[k, dist - 1, d], recv_sem=fr.at[k, dist - 1, d],
             device_id={"mp": x * 2 + 1 - c}, device_id_type=MESH)
 
     def when(cond, f):
@@ -99,7 +128,7 @@
 
     can = {True: z < nz - 1, False: z > 0}
 
-    for a in range(2):
+    for a in (1, 0):
         for right in (True, False):
             when(can[right], lambda a=a, right=right: zsend(a, 0, right).start())
     for a in range(2):
@@ -112,7 +141,7 @@
         return z - dist >= 0 if right else z + dist <= nz - 1
 
     def zstep(dist):
-        for a in range(2):
+        for a in (1, 0):
             for right in (True, False):
                 k = 0 if right else 1
 
@@ -122,27 +151,50 @@
                         when(can[right], lambda: zsend(a, dist, right).start())
                     for d in range(1, nx):
                         xcopy(a, k, dist, d, right, True).start()
+                    if a == 1 and split:
+                        ycopy(k, dist, 0, right, True).start()
                     ccopy(a, k, dist, 0, right, True).start()
 
                 when(has(dist, right), got)
 
     def xstep(dist):
-        for a in range(2):
+        for a in (1, 0):
             for right in (True, False):
                 k = 0 if right else 1
 
                 def got(a=a, right=right, k=k):
                     for d in range(1, nx):
                         xcopy(a, k, dist, d, right, False).wait_recv()
+                        if a == 1 and split:
+                            ycopy(k, dist, d, right, True).start()
                         ccopy(a, k, dist, d, right, True).start()
 
                 when(has(dist, right), got)
 
+    def ystep(dist, ds):
+        if not split or dist < 1:
+            return
+        for right in (True, False):
+            k = 0 if right else 1
+
+            def got(right=right, k=k):
+                for d in ds:
+                    ycopy(k, dist, d, right, False).wait_recv()
+                    fcopy(k, dist, d, right, True).start()
+
+            when(has(dist, right), got)
+
+    far = tuple(range(1, nx))
     for dist in range(1, nz):
         zstep(dist)
         if dist > 1:
             xstep(dist - 1)
+        ystep(dist - 1, (0,))
+        ystep(dist - 2, far)
+    ystep(nz - 2, far)
+    ystep(nz - 1, (0,))
     xstep(nz - 1)
+    ystep(nz - 1, far)
 
     for a in range(2):
         pltpu.make_async_copy(
@@ -161,6 +213,10 @@
                         for d in range(nx):
                             ccopy(a, k, dist, d, right, True).wait_send()
                             ccopy(a, k, dist, d, right, False).wait_recv()
+                            if a == 1 and split:
+                                ycopy(k, dist, d, right, True).wait_send()
+                                fcopy(k, dist, d, right, True).wait_send()
+                                fcopy(k, dist, d, right, False).wait_recv()
                     when(has(dist, right), fin)
 
 
@@ -170,6 +226,7 @@
     dma = pltpu.SemaphoreType.DMA
     anyspec = pl.BlockSpec(memory_space=pl.ANY)
     shape = jax.ShapeDtypeStruct((nz * rows, width), bf16)
+    ex = (2, nz - 1, nx) if halves(rows, nm) else (1,)
     return pl.pallas_call(
         functools.partial(gather_kernel, nz, nm),
         out_shape=(shape, shape),
@@ -181,6 +238,7 @@
             dma((2, 2, nz)), dma((2, 2, nz)),
             dma((2, 2, nz - 1, nx)), dma((2, 2, nz - 1, nx)),
             dma((2, 2, nz - 1, nx)), dma((2, 2, nz - 1, nx)),
+            dma(ex), dma(ex), dma(ex), dma(ex),
         ],
         compiler_params=pltpu.CompilerParams(collective_id=0, has_side_effects=True),
         name="gather_inputs",
@@ -236,6 +294,8 @@
         wide = heads * vd
         for i in range(rows // chunk):
             rr = slice(i * chunk, (i + 1) * chunk)
+            if i == 1:
+                share_mix(nz, nm, mix, mix_all, xs, xr, ys, yr, cs, cr, os, orr, 2)
             res = []
             for h in range(heads):
                 lo = (h * vd) // 128 * 128
@@ -275,10 +335,11 @@
     m = lax.axis_index("mp")
     g = lax.axis_index("groups")
     x, c = m // 2, m % 2
-    size = mix.shape[0] // 4
+    n = 4 if mix.shape[0] % 128 == 0 else 2
+    size = mix.shape[0] // (2 * n)
 
     def rows(gg, p):
-        return pl.ds(pl.multiple_of((gg * 2 + p) * size, size), size)
+        return pl.ds(pl.multiple_of((gg * n + p) * size, size), size)
 
     def xcopy(p, d, mine):
         o = lax.rem(x + d, nx) if mine else lax.rem(x - d + nx, nx)
@@ -310,6 +371,17 @@
             src_ref=mix, dst_ref=mix_all.at[m if mine else x * 2 + 1 - c],
             send_sem=os, recv_sem=orr,
             device_id={"mp": x * 2 + 1 - c}, device_id_type=MESH)
+
+    def pass_on(p):
+        for d in range(1, nx):
+            xcopy(p, d, False).wait_recv()
+            ycopy(p, d, True).start()
+            ccopy(p, d, False, True).start()
+
+    def bring(p):
+        for d in range(1, nx):
+            ycopy(p, d, False).wait_recv()
+            ccopy(p, d, True, True).start()
 
     if phase == 0:
         @pl.when(step == 0)
@@ -320,28 +392,31 @@
             pl.semaphore_signal(barrier, inc=1, device_id={"mp": x * 2 + 1 - c}, device_id_type=MESH)
             pl.semaphore_signal(barrier, inc=1, device_id={"groups": 1 - g}, device_id_type=MESH)
             pl.semaphore_wait(barrier, nx + 1)
-            for p in range(2):
+            for p in range(n):
                 for d in range(1, nx):
                     xcopy(p, d, True).start()
             own(True).start()
 
-        for p in range(2):
-            @pl.when(step == nz + 2 * p)
-            def _(p=p):
-                for d in range(1, nx):
-                    xcopy(p, d, False).wait_recv()
-                    ycopy(p, d, True).start()
-                    ccopy(p, d, False, True).start()
+        turns = {4: (nz - 1, None, nz, nz + 2), 2: (nz, nz + 2)}[n]
+        for p in range(n):
+            if turns[p] is not None:
+                pl.when(step == turns[p])(functools.partial(pass_on, p))
+
+        @pl.when(step == 2 * nz - 1)
+        def _():
+            for p in range(n // 2):
+                bring(p)
+    elif phase == 2:
+        if n == 4:
+            pl.when(step == nz - 1)(functools.partial(pass_on, 1))
     else:
         @pl.when(step == 2 * nz - 1)
         def _():
-            for p in range(2):
-                for d in range(1, nx):
-                    ycopy(p, d, False).wait_recv()
-                    ccopy(p, d, True, True).start()
+            for p in range(n // 2, n):
+                bring(p)
             own(True).wait_send()
             own(False).wait_recv()
-            for p in range(2):
+            for p in range(n):
                 for d in range(1, nx):
                     xcopy(p, d, True).wait_send()
                     ycopy(p, d, True).wait_send()
@@ -377,8 +452,8 @@
             pltpu.VMEM((rows, heads * qk), bf16),
             pltpu.VMEM((s_all, heads * qk), bf16),
             pltpu.VMEM((s_all, heads * vd), bf16),
-            dma((2, nx)), dma((2, nx)), dma((2, nx)), dma((2, nx)),
-            dma((2, nx, 2)), dma((2, nx, 2)), dma, dma,
+            dma((4, nx)), dma((4, nx)), dma((4, nx)), dma((4, nx)),
+            dma((4, nx, 2)), dma((4, nx, 2)), dma, dma,
         ],
         compiler_params=pltpu.CompilerParams(
             collective_id=2, has_side_effects=True, vmem_limit_bytes=56 << 20),

time: 117 us -> 109 us (0.932)
  Pallas kernels: 113 us -> 104 us
    pallas_call x1, Pallas kernels: 54 us -> 45.7 us  [gather_inputs(): pl.pallas_call(functools.partial(gather_kernel, nz, nm), out_shape=(shape...]
where the time goes in v3:
time: 109 us; the launch traced here: 108 us
  Pallas kernels  104 us (95%)
  local copies, waits for them, and re-layouts  3.12 us (3%)
    pallas_call x1, Pallas kernels, gather_inputs(): pl.pallas_call(functools.partial(gather_kernel, nz, nm), out_shape=(shape...  45.7 us
    pallas_call x1, Pallas kernels, attend(): pl.pallas_call(functools.partial(attend_kernel, nz, nm, heads, qk, vd), g...  29.6 us
    pallas_call x1, Pallas kernels, tail(): pl.pallas_call(functools.partial(tail_kernel, nz, nm), out_shape=jax.Shap...  29.2 us

profile of v3, /device:TPU:0, one launch (start us, length us, event | category | flops | bytes accessed | tf_op | source)
XLA Modules:
  0.0 107.7 jit_solution(12384040257868369347)
XLA Ops:
  0.0 0.0 copy-start
  0.0 45.7 %gather_inputs.1 = (bf16[1536,1536]{1,0:T(8,128)(2,1)}, bf16[1536,1536]{1,0:T(8,128)(2,1)}) custom-call(bf16[384,1536]{1,0:T(8,128)(2,1)} %nuc_h.1, bf16[384,1536]{1,0:T(8,128)(2,1)} %loc_h.1), custom_call_target="tpu_custom_call" | custom-call | tf_op jit(solution)/shard_map/gather_inputs/pallas_call | solution.py:230
  45.7 0.0 copy-done
  45.7 0.6 reshape.6.gain
  46.3 0.0 copy-start.1
  46.3 29.6 %attend.1 = (bf16[2,384,384]{2,1,0:T(8,128)(2,1)}, bf16[4,384,1536]{2,1,0:T(8,128)(2,1)}) custom-call(f32[2]{0:T(128)} %sharp.1, bf16[1536,1536]{1,0:T(8,128)(2,1)} %get-tuple-element.9.nuc, bf16[1536,1536]{1,0:T(8,128)(2,1)} %get-tuple-element.10.loc.loc_all, f32[1,1536]{1,0:T(1,128)} %reshape.6.gain, bf16[2,1536,256]{2,1,0:T(8,128)(2,1)} %wqk.1, ...), custom_call_target="tpu_custom_call" | custom-call | tf_op jit(solution)/shard_map/attend/pallas_call | solution.py:439
  75.9 0.0 copy-done.1
  75.9 0.6 reshape.7.gain
  76.5 29.2 %tail.1 = f32[384,384]{1,0:T(8,128)} custom-call(bf16[2,384,384]{2,1,0:T(8,128)(2,1)} %get-tuple-element.11.att, bf16[384,1536]{1,0:T(8,128)(2,1)} %nuc_h.1, bf16[384,1536]{1,0:T(8,128)(2,1)} %loc_h.1, bf16[1536,1536]{1,0:T(8,128)(2,1)} %get-tuple-element.10.loc.loc_all, f32[1,1536]{1,0:T(1,128)} %reshape.7.gain, bf16[384,1536]{1,0:T(8,128)(2,1)} %mix.3, ...), custom_call_target="tpu_custom_call" | custom-call | tf_op jit(solution)/shard_map/tail/pallas_call | solution.py:586
  105.7 1.9 %copy.12 = f32[384,384]{1,0:T(8,128)} copy(f32[384,384]{1,0:T(8,128)} %tail.1) | data formatting | bytes 1179648
Async XLA Ops:
  0.0 45.7 %copy-start = (f32[1536]{0:T(1024)S(1)}, f32[1536]{0:T(1024)}, u32[]{:S(2)}) copy-start(f32[1536]{0:T(1024)} %param.12) | copy-start | bytes 18436
  46.3 29.6 %copy-start.1 = (f32[1536]{0:T(1024)S(1)}, f32[1536]{0:T(1024)}, u32[]{:S(2)}) copy-start(f32[1536]{0:T(1024)} %param.17) | copy-start | bytes 18436
